TPU v7x, 32 devices: a whole 2x2x4 slice. The times are simulated.
32 devices in a mesh: groups: 2 (over x), sensor: 16 (over z, y, core).
Axes of the slice: x: 2, y: 2, z: 4, core: 2. Of those that a mesh axis runs over, the one named last changes fastest.
Arguments:
- series: float32 [288, 1536], P(None, ('groups', 'sensor')), parts along dimension 1, may hold values from -6 to 6
- starts: int32 [2], P('groups'), parts along dimension 0, may hold values from 0 to 276
- sensor_order: int32 [1536], P(('groups', 'sensor')), parts along dimension 0, may hold values from 0 to 767, each once
- emb_src: float32 [10, 1536], P(None, ('groups', 'sensor')), parts along dimension 1, may hold values from -4.4 to 330
- emb_dst: float32 [10, 1536], P(None, ('groups', 'sensor')), parts along dimension 1, may hold values from -4.4 to 4.4
- start_proj: float32 [2, 32], replicated, may hold values from -4 to 4
- conv_weight: bfloat16 [64, 64], replicated, may hold values from -0.75 to 0.75
- mix_weight: bfloat16 [96, 32], replicated, may hold values from -0.625 to 0.625
- out_grad: bfloat16 [1536, 384], P(('groups', 'sensor')), parts along dimension 0, may hold values from -0.59765625 to 0.59765625
Outputs:
- layer_out: bfloat16 [1536, 384], P(('groups', 'sensor')), parts along dimension 0
- grad_src: float32 [10, 1536], P(None, ('groups', 'sensor')), parts along dimension 1
- grad_dst: float32 [10, 1536], P(None, ('groups', 'sensor')), parts along dimension 1
- grad_mix: float32 [192, 32], P('groups'), parts along dimension 0
There are 2 independent parts, one for each index of `groups`. A program takes and returns all parts, laid end to end along the dimension named above; an argument that names none is the same for every part. Nothing has to cross between parts.
All inputs are finite; a program needn't handle non-finite values.
Results may differ from a plain program's by a relative error of at most 0.035.
Values may be sent and summed in bfloat16 or wider, within the bound.
A program may use at most 64 MiB of HBM per device.

v0:
```python
import math
import jax
import jax.numpy as jnp
from jax import lax
from jax.sharding import PartitionSpec as P

STEPS = 12
highest = lax.Precision.HIGHEST


def front(readings, start_proj, conv_weight):
    sensors_here = readings.shape[0]
    channels = start_proj.shape[1]
    padded = jnp.concatenate(
        [jnp.zeros(readings.shape[:-1] + (1,), jnp.float32), readings], axis=-1
    )
    inputs = (padded[..., None] * start_proj[0] + start_proj[1]).astype(jnp.bfloat16)
    paired = jnp.concatenate([inputs[:, :, :-1, :], inputs[:, :, 1:, :]], axis=-1).reshape(
        -1, 2 * channels
    )
    gate_terms = jnp.dot(paired, conv_weight, preferred_element_type=jnp.float32)
    hidden = (jnp.tanh(gate_terms[:, :channels]) * jax.nn.sigmoid(gate_terms[:, channels:])).astype(
        jnp.bfloat16
    )
    return (hidden.reshape(sensors_here, -1), inputs[:, :, 1:, :].reshape(sensors_here, -1))


def mixing(residual, hidden, diffused, second, mix_weight):
    channels = mix_weight.shape[1]
    stacked = jnp.concatenate(
        [member.reshape(-1, channels) for member in (hidden, diffused, second)], axis=1
    )
    summed = residual.reshape(-1, channels).astype(jnp.float32) + jnp.dot(
        stacked, mix_weight, preferred_element_type=jnp.float32
    )
    return (summed.astype(jnp.bfloat16).reshape(hidden.shape[0], -1), stacked)


def channel_grads(out_grad, mix_weight):
    channels = mix_weight.shape[1]
    row_count = out_grad.shape[0]
    flat_grad = out_grad.reshape(-1, channels)
    dims = (((1,), (1,)), ((), ()))
    grad_once = lax.dot_general(
        flat_grad, mix_weight[channels : 2 * channels], dims, preferred_element_type=jnp.float32
    )
    grad_twice = lax.dot_general(
        flat_grad, mix_weight[2 * channels :], dims, preferred_element_type=jnp.float32
    )
    return (
        grad_once.astype(jnp.bfloat16).reshape(row_count, -1),
        grad_twice.astype(jnp.bfloat16).reshape(row_count, -1),
    )


def tile_probs(rows_emb, cols_emb, row_max, row_total):
    scores = jnp.einsum("ei,ej->ij", rows_emb, cols_emb, precision=highest)
    shares = jnp.exp(jnp.maximum(scores, 0.0) - row_max[:, None]) / row_total[:, None]
    return (scores, shares)


def pair_dot(left, right):
    return lax.dot_general(
        left, right, (((1,), (1,)), ((), ())), preferred_element_type=jnp.float32
    )


def in_blocks(step_fn, status, members, axis_dim):
    amount = members[0].shape[axis_dim]
    span_size = math.gcd(amount, 512)

    def advance(position, current):
        opening = position * span_size
        sliced = tuple(
            (lax.dynamic_slice_in_dim(member, opening, span_size, axis_dim) for member in members)
        )
        return step_fn(current, sliced, opening)

    return lax.fori_loop(0, amount // span_size, advance, status)


def score_grads(status, emb_src, cols_dst, offset, scores, shares, dweights):
    grad_rows, grad_cols = status
    dscore = jnp.where(scores > 0.0, shares * dweights, 0.0)
    grad_rows = grad_rows + jnp.einsum("ej,ij->ei", cols_dst, dscore, precision=highest)
    span_size = dscore.shape[1]
    current = lax.dynamic_slice_in_dim(grad_cols, offset, span_size, 1)
    added = current + jnp.einsum("ei,ij->ej", emb_src, dscore, precision=highest)
    return (grad_rows, lax.dynamic_update_slice_in_dim(grad_cols, added, offset, 1))


def per_device(
    series, starts, sensor_order, emb_src, emb_dst, start_proj, conv_weight, mix_weight, out_grad
):
    local_rows = sensor_order.shape[0]
    embed_dim = emb_src.shape[0]
    channels = start_proj.shape[1]
    all_rows = local_rows * lax.axis_size("sensor")
    windows = jax.vmap(lambda first_step: lax.dynamic_slice_in_dim(series, first_step, STEPS, 0))(
        starts
    )
    flat_windows = windows.reshape(-1, local_rows)
    window_rows = flat_windows.shape[0]

    def pick_step(status, members, offset):
        readings_sum, dst_all = status
        block_windows, block_dst = members
        span_size = block_windows.shape[1]
        onehot = (sensor_order[:, None] == offset + lax.iota(jnp.int32, span_size)[None, :]).astype(
            jnp.float32
        )
        readings_sum = readings_sum + jnp.einsum(
            "wj,pj->wp", block_windows, onehot, precision=highest
        )
        return (readings_sum, lax.dynamic_update_slice_in_dim(dst_all, block_dst, offset, 1))

    readings_sum, dst_all = in_blocks(
        pick_step,
        (
            jnp.zeros((window_rows, local_rows), jnp.float32),
            jnp.zeros((embed_dim, all_rows), jnp.float32),
        ),
        (
            lax.all_gather(flat_windows, "sensor", axis=1, tiled=True),
            lax.all_gather(emb_dst, "sensor", axis=1, tiled=True),
        ),
        1,
    )
    readings = readings_sum.T.reshape(local_rows, -1, STEPS)
    hidden, residual = front(readings, start_proj, conv_weight)
    feat_cols = hidden.shape[1]
    span_all = math.gcd(all_rows, 512)

    def stat_step(position, current):
        best_score, summed = current
        cols_dst = lax.dynamic_slice_in_dim(dst_all, position * span_all, span_all, 1)
        scores = jnp.maximum(jnp.einsum("ei,ej->ij", emb_src, cols_dst, precision=highest), 0.0)
        new_best = jnp.maximum(best_score, jnp.max(scores, axis=1))
        summed = summed * jnp.exp(best_score - new_best) + jnp.sum(
            jnp.exp(scores - new_best[:, None]), axis=1
        )
        return (new_best, summed)

    row_max, row_total = lax.fori_loop(
        0,
        all_rows // span_all,
        stat_step,
        (jnp.zeros((local_rows,), jnp.float32), jnp.zeros((local_rows,), jnp.float32)),
    )
    grad_once, grad_twice = channel_grads(out_grad, mix_weight)

    def spread_step(status, members, offset):
        block_feat = members[0]
        cols_dst = lax.dynamic_slice_in_dim(dst_all, offset, block_feat.shape[0], 1)
        scores, shares = tile_probs(emb_src, cols_dst, row_max, row_total)
        return status + jnp.dot(
            shares.astype(jnp.bfloat16), block_feat, preferred_element_type=jnp.float32
        )

    first_init = jnp.zeros((local_rows, feat_cols), jnp.float32)
    first_result = in_blocks(
        spread_step, first_init, (lax.all_gather(hidden, "sensor", axis=0, tiled=True),), 0
    )
    diffused = first_result.astype(jnp.bfloat16)

    def plain_step(status, members, offset):
        accumulated, grad_rows, grad_cols = status
        return (spread_step(accumulated, members, offset), grad_rows, grad_cols)

    second_init = (
        jnp.zeros((local_rows, feat_cols), jnp.float32),
        jnp.zeros((embed_dim, local_rows), jnp.float32),
        jnp.zeros((embed_dim, all_rows), jnp.float32),
    )
    second_result = in_blocks(
        plain_step, second_init, (lax.all_gather(diffused, "sensor", axis=0, tiled=True),), 0
    )
    second_full, grad_rows, grad_cols = second_result
    second = second_full.astype(jnp.bfloat16)
    layer_out, stacked = mixing(residual, hidden, diffused, second, mix_weight)
    mix_part = lax.dot_general(
        stacked,
        out_grad.reshape(-1, channels),
        (((0,), (0,)), ((), ())),
        preferred_element_type=jnp.float32,
    )
    span_size = math.gcd(lax.axis_size("sensor") * local_rows, 512)

    def piece_term(position):
        cols_dst = lax.dynamic_slice_in_dim(dst_all, position * span_size, span_size, 1)
        scores, shares = tile_probs(emb_src, cols_dst, row_max, row_total)
        return lax.dot_general(
            shares.astype(jnp.bfloat16),
            grad_twice,
            (((0,), (0,)), ((), ())),
            preferred_element_type=jnp.float32,
        )

    adjoint_sum = lax.psum_scatter(
        lax.map(
            piece_term,
            jnp.arange(lax.axis_size("sensor") * local_rows // span_size, dtype=jnp.int32),
        ).reshape(lax.axis_size("sensor") * local_rows, -1),
        "sensor",
        scatter_dimension=0,
        tiled=True,
    )
    carried = (grad_once.astype(jnp.float32) + adjoint_sum).astype(jnp.bfloat16)
    row_delta = jnp.sum(
        grad_twice.astype(jnp.float32) * second_full + carried.astype(jnp.float32) * first_result,
        axis=1,
    )

    def pair_step(status, members, offset):
        block_hidden, block_diff = members
        cols_dst = lax.dynamic_slice_in_dim(dst_all, offset, block_hidden.shape[0], 1)
        scores, shares = tile_probs(emb_src, cols_dst, row_max, row_total)
        dweights = (
            pair_dot(grad_twice, block_diff) + pair_dot(carried, block_hidden) - row_delta[:, None]
        )
        return score_grads(status, emb_src, cols_dst, offset, scores, shares, dweights)

    grad_rows, grad_cols = in_blocks(
        pair_step,
        (grad_rows, grad_cols),
        (
            lax.all_gather(hidden, "sensor", axis=0, tiled=True),
            lax.all_gather(diffused, "sensor", axis=0, tiled=True),
        ),
        0,
    )
    grad_dst = lax.psum_scatter(grad_cols, "sensor", scatter_dimension=1, tiled=True)
    grad_mix = lax.psum(mix_part, "sensor")
    return (layer_out, grad_rows, grad_dst, grad_mix)


def solution(mesh):
    placed = (
        P(None, ("groups", "sensor")),
        P("groups"),
        P(("groups", "sensor")),
        P(None, ("groups", "sensor")),
        P(None, ("groups", "sensor")),
        P(),
        P(),
        P(),
        P(("groups", "sensor"), None),
    )
    return jax.shard_map(
        per_device,
        mesh=mesh,
        in_specs=placed,
        out_specs=(
            P(("groups", "sensor"), None),
            P(None, ("groups", "sensor")),
            P(None, ("groups", "sensor")),
            P("groups", None),
        ),
        check_vma=False,
    )
```

profile of v0, /device:TPU:0, one launch (start us, length us, event | category | flops | bytes accessed | tf_op | source)
XLA Modules:
  0.0 194.4 jit_solution(2964574075094498716)
XLA Ops:
  8.2 23.4 %all-gather = f32[16,48,12]{1,2,0:T(8,128)S(1)} all-gather(f32[1,48,12]{1,2,0:T(8,128)S(1)} %bitcast.98), channel_id=1, replica_groups=mesh['groups'=2,'sensor'=16] {'sensor'}, dimensions={0}, use_global_device_ids=true | all-gather | bytes 39168 | tf_op jit(solution)/shard_map/all_gather | solution.py:124
  31.8 18.0 %all-gather.1 = f32[16,48,10]{1,2,0:T(8,128)S(1)} all-gather(f32[1,48,10]{1,2,0:T(8,128)} %bitcast.100), channel_id=1, replica_groups=mesh['groups'=2,'sensor'=16] {'sensor'}, dimensions={0}, use_global_device_ids=true | all-gather | bytes 32640 | tf_op jit(solution)/shard_map/all_gather | solution.py:125
  50.0 2.7 %while.88 = (s32[]{:T(128)}, f32[12,48]{1,0:T(8,128)S(1)}, f32[10,768]{1,0:T(8,128)S(1)}, f32[12,768]{1,0:T(8,128)S(1)}, s32[48]{0:T(128)}, /*index=5*/f32[10,76...) while((s32[]{:T(128)}, f32[12,48]{1,0:T(8,128)S(1)}, f32[10,768]{1,0:T(8,128)S(1)}, ...), condition=%wide.region_1.0_spmd.clone, body=%wide.region_0.0_spmd.clone.sunk | while | flops 1783175 | bytes 62065 | solution.py:79
  50.0 0.8 convolution_add_fusion.10
  50.9 0.8 convolution_add_fusion.10
  51.9 0.8 convolution_add_fusion.10
  52.7 1.8 while.89
  52.8 0.3 fusion.128
  53.4 0.3 fusion.128
  53.9 0.3 fusion.128
  54.7 0.3 convolution_convert_fusion.1
  55.3 7.5 %while.87 = (s32[]{:T(128)}, f32[3,256,384]{2,1,0:T(8,128)}, s32[3]{0:T(128)S(1)}, f32[10,768]{1,0:T(8,128)S(1)}, f32[10,48]{1,0:T(8,128)S(1)}, /*index=5*/f32[4...) while((s32[]{:T(128)}, f32[3,256,384]{2,1,0:T(8,128)}, ...), condition=%wide.region_11.12_spmd, body=%wide.region_10.11_spmd.sunk | while | flops 10960902 | bytes 505023 | solution.py:200
  55.3 0.6 dynamic_slice.136
  56.8 1.0 fusion.124
  57.8 0.6 dynamic_slice.136
  59.3 1.0 fusion.124
  60.3 0.6 dynamic_slice.136
  61.5 0.3 fusion.123
  61.8 1.0 fusion.124
  62.9 0.6 copy-done.6
  64.2 0.3 copy-done.5
  65.1 20.4 %all_gather.16 = bf16[768,384]{1,0:T(8,128)(2,1)S(1)} all-gather(bf16[48,384]{1,0:T(8,128)(2,1)S(1)} %reshape.86), channel_id=1, replica_groups=mesh['groups'=2,'sensor'=16] {'sensor'}, dimensions={0}, use_global_device_ids=true | all-gather | bytes 626688 | tf_op jit(solution)/shard_map/all_gather | solution.py:162
  85.5 1.4 while.90
  87.7 20.1 %all_gather.17 = bf16[768,384]{1,0:T(8,128)(2,1)S(1)} all-gather(bf16[48,384]{1,0:T(8,128)(2,1)S(1)} %convert_element_type.68), channel_id=1, replica_groups=mesh['groups'=2,'sensor'=16] {'sensor'}, dimensions={0}, use_global_device_ids=true | all-gather | bytes 626688 | tf_op jit(solution)/shard_map/all_gather | solution.py:176
  107.9 1.4 while.91
  109.2 12.6 %reduce-scatter.5.cloned.1.call-done = f32[48,384]{1,0:T(8,128)} async-done(((f32[768,384]{1,0:T(8,128)}), f32[48,384]{1,0:T(8,128)}) %reduce-scatter.5.cloned.1.call-update) | async-done | bytes 73744 | tf_op jit(solution)/shard_map/reduce_scatter | solution.py:199
  121.9 1.0 add_reduce_fusion
  123.2 3.0 %while.92 = (s32[]{:T(128)}, f32[10,48]{1,0:T(8,128)S(1)}, f32[10,768]{1,0:T(8,128)S(1)}, f32[10,768]{1,0:T(8,128)S(1)}, f32[10,48]{1,0:T(8,128)S(1)}, /*index=5...) while((s32[]{:T(128)}, f32[10,48]{1,0:T(8,128)S(1)}, ...), condition=%wide.region_15.16_spmd.clone, body=%wide.region_14.15_spmd.clone.sunk | while | flops 23399876 | bytes 904809 | solution.py:79
  126.2 0.9 copy.46
  127.7 0.8 reshape.89
  128.5 57.7 %psum.7 = f32[96,32]{0,1:T(8,128)} all-reduce(f32[96,32]{0,1:T(8,128)S(1)} %fusion.55), channel_id=1, replica_groups=mesh['groups'=2,'sensor'=16] {'sensor'}, use_global_device_ids=true, to_apply=%region_17.18 | all-reduce | flops 3072 | bytes 24576 | tf_op jit(solution)/shard_map/psum | solution.py:233
  186.1 1.4 copy.47
  (107 shorter events, 10.7 us)
Async XLA Ops:
  7.2 0.9 copy-start
  7.2 45.6 %copy-start.1 = (f32[10,48]{1,0:T(8,128)S(1)}, f32[10,48]{1,0:T(8,128)}, u32[]{:S(2)}) copy-start(f32[10,48]{1,0:T(8,128)} %param.24) | copy-start | bytes 5764
  7.2 114.7 %reduce-scatter.5.cloned.1.call-start = ((), (), s32[]{:S(2)}) async-start(), calls=%async_computation.2 | async-start | bytes 1253376 | tf_op jit(solution)/shard_map/reduce_scatter | solution.py:199
  31.7 22.8 %copy-start.3 = (bf16[48,384]{1,0:T(8,128)(2,1)S(1)}, bf16[48,384]{1,0:T(8,128)(2,1)}, u32[]{:S(2)}) copy-start(bf16[48,384]{1,0:T(8,128)(2,1)} %param.29) | copy-start | bytes 110596
  31.8 22.9 %copy-start.4 = (bf16[96,32]{0,1:T(8,128)(2,1)S(1)}, bf16[96,32]{0,1:T(8,128)(2,1)}, u32[]{:S(2)}) copy-start(bf16[96,32]{0,1:T(8,128)(2,1)} %param.28) | copy-start | bytes 18436
  62.8 0.7 copy-start.6
  62.8 123.3 %reduce-scatter.7.cloned.1.call-start = ((), (), s32[]{:S(2)}) async-start(), calls=%async_computation.3 | async-start | bytes 417792
  63.8 0.7 copy-start.5
  126.2 61.3 %copy-start.2 = (f32[10,48]{1,0:T(8,128)}, f32[10,48]{1,0:T(8,128)S(1)}, u32[]{:S(2)}) copy-start(f32[10,48]{1,0:T(8,128)S(1)} %get-tuple-element.696) | copy-start | bytes 5764
Sparse Core Ops, SparseCore 0:
  62.9 58.8 reduce-scatter.4
  127.3 54.7 reduce-scatter.6
where the time goes:
time: 195 us; the launch traced here: 194 us
  blocking collectives  140 us (72%)
  between operations  15 us (8%)
  matrix products  13.9 us (7%)
  waiting for transfers between devices  12.7 us (7%)
  local copies, waits for them, and re-layouts  8.47 us (4%)
  loops' own time  2.58 us (1%)
  other arithmetic  2.1 us (1%)
    psum x1, blocking collectives, per_device(): grad_mix = lax.psum(mix_part, 'sensor')  57.7 us
    all_gather x1, blocking collectives, per_device(): lax.all_gather(flat_windows, 'sensor', axis=1, tiled=True)  23.4 us
    all_gather x1, blocking collectives, per_device(): lax.all_gather(hidden, 'sensor', axis=0, tiled=True)  20.4 us
    all_gather x1, blocking collectives, per_device(): lax.all_gather(diffused, 'sensor', axis=0, tiled=True)  20.1 us
    all_gather x1, blocking collectives, per_device(): lax.all_gather(emb_dst, 'sensor', axis=1, tiled=True)  18 us
    reduce_scatter x1, waiting for transfers between devices, per_device(): lax.psum_scatter(lax.map(piece_term, jnp.arange(lax.axis_size('sensor') *...  12.6 us
  transfers between devices with their start and end apart: 2, of which 1 were waited for; matrix products, arithmetic and copies ran while one was open for 3% of the time, Pallas kernels for 0%

commit v1 on v0

--- a/solution.py
+++ b/solution.py
@@ -172,9 +172,26 @@
         jnp.zeros((embed_dim, local_rows), jnp.float32),
         jnp.zeros((embed_dim, all_rows), jnp.float32),
     )
-    second_result = in_blocks(
-        plain_step, second_init, (lax.all_gather(diffused, "sensor", axis=0, tiled=True),), 0
-    )
+
+    def weights_convert(m, axis_tag):
+        latest = lax.axis_size(axis_tag)
+        q_next = lax.axis_index(axis_tag)
+        block_last, extra = (latest, q_next)
+        passed, b_now = (m, 1)
+        while b_now < block_last:
+            crops = []
+            num = 0
+            while num < block_last:
+                crops.append((num, num ^ b_now))
+                num = num + 1
+            oldest = lax.ppermute(passed, axis_tag, crops)
+            formed = jnp.concatenate([passed, oldest], 0)
+            piece_now = jnp.concatenate([oldest, passed], 0)
+            passed = jnp.where(extra & b_now == 0, formed, piece_now)
+            b_now = 2 * b_now
+        return passed
+
+    second_result = in_blocks(plain_step, second_init, (weights_convert(diffused, "sensor"),), 0)
     second_full, grad_rows, grad_cols = second_result
     second = second_full.astype(jnp.bfloat16)
     layer_out, stacked = mixing(residual, hidden, diffused, second, mix_weight)

time: 195 us -> 221 us (1.13)
  waiting for transfers between devices: 12.7 us -> 35 us
  blocking collectives: 140 us -> 143 us
    reduce_scatter x1, waiting for transfers between devices: 12.6 us -> 30.6 us  [per_device(): lax.psum_scatter(lax.map(piece_term, jnp.arange(lax.axis_size('sensor') *...]
    ppermute x0 -> x4, waiting for transfers between devices: none -> 4.3 us  [weights_convert(): oldest = lax.ppermute(passed, axis_tag, crops)]
    all_gather x1, blocking collectives: 20.1 us -> 23.2 us  [per_device(): lax.all_gather(diffused, 'sensor', axis=0, tiled=True)]
  transfers between devices with their start and end apart: 2 -> 6, of which waited for: 1 -> 3; matrix products, arithmetic and copies ran while one was open for 3% -> 5% of each run, Pallas kernels for 0% -> 0%
where the time goes in v1:
time: 221 us
  blocking collectives  143 us (65%)
  waiting for transfers between devices  35 us (16%)
  between operations  15.1 us (7%)
  matrix products  13.8 us (6%)
  local copies, waits for them, and re-layouts  8.2 us (4%)
  loops' own time  2.6 us (1%)
  other arithmetic  2.43 us (1%)
    psum x1, blocking collectives, per_device(): grad_mix = lax.psum(mix_part, 'sensor')  57.8 us
    reduce_scatter x1, waiting for transfers between devices, per_device(): lax.psum_scatter(lax.map(piece_term, jnp.arange(lax.axis_size('sensor') *...  30.6 us
    all_gather x1, blocking collectives, per_device(): lax.all_gather(flat_windows, 'sensor', axis=1, tiled=True)  23.4 us
    all_gather x1, blocking collectives, per_device(): lax.all_gather(diffused, 'sensor', axis=0, tiled=True)  23.2 us
    all_gather x1, blocking collectives, per_device(): lax.all_gather(hidden, 'sensor', axis=0, tiled=True)  20.4 us
    all_gather x1, blocking collectives, per_device(): lax.all_gather(emb_dst, 'sensor', axis=1, tiled=True)  18 us
  transfers between devices with their start and end apart: 6, of which 3 were waited for; matrix products, arithmetic and copies ran while one was open for 5% of the time, Pallas kernels for 0%

profile of v1, /device:TPU:0, one launch (start us, length us, event | category | flops | bytes accessed | tf_op | source)
XLA Modules:
  0.0 221.0 jit_solution(16845264735012282721)
XLA Ops:
  7.3 0.8 slice_bitcast_fusion.1
  8.8 23.4 %all-gather = f32[16,48,12]{1,2,0:T(8,128)S(1)} all-gather(f32[1,48,12]{1,2,0:T(8,128)S(1)} %bitcast.98), channel_id=1, replica_groups=mesh['groups'=2,'sensor'=16] {'sensor'}, dimensions={0}, use_global_device_ids=true | all-gather | bytes 39168 | tf_op jit(solution)/shard_map/all_gather | solution.py:124
  32.4 18.0 %all-gather.1 = f32[16,48,10]{1,2,0:T(8,128)S(1)} all-gather(f32[1,48,10]{1,2,0:T(8,128)} %bitcast.100), channel_id=1, replica_groups=mesh['groups'=2,'sensor'=16] {'sensor'}, dimensions={0}, use_global_device_ids=true | all-gather | bytes 32640 | tf_op jit(solution)/shard_map/all_gather | solution.py:125
  50.6 2.7 %while.88 = (s32[]{:T(128)}, f32[12,48]{1,0:T(8,128)S(1)}, f32[10,768]{1,0:T(8,128)S(1)}, f32[12,768]{1,0:T(8,128)S(1)}, s32[48]{0:T(128)}, /*index=5*/f32[10,76...) while((s32[]{:T(128)}, f32[12,48]{1,0:T(8,128)S(1)}, f32[10,768]{1,0:T(8,128)S(1)}, ...), condition=%wide.region_1.0_spmd.clone, body=%wide.region_0.0_spmd.clone.sunk | while | flops 1783175 | bytes 62065 | solution.py:79
  50.7 0.8 convolution_add_fusion.10
  51.6 0.8 convolution_add_fusion.10
  52.5 0.8 convolution_add_fusion.10
  53.8 1.8 while.89
  53.8 0.3 fusion.128
  54.4 0.3 fusion.128
  56.3 20.4 %all_gather.15 = bf16[768,384]{1,0:T(8,128)(2,1)S(1)} all-gather(bf16[48,384]{1,0:T(8,128)(2,1)S(1)} %reshape.86), channel_id=1, replica_groups=mesh['groups'=2,'sensor'=16] {'sensor'}, dimensions={0}, use_global_device_ids=true | all-gather | bytes 626688 | tf_op jit(solution)/shard_map/all_gather | solution.py:162
  76.7 1.4 while.90
  78.1 0.4 collective-permute-start
  78.7 0.7 collective-permute-done
  79.4 0.4 collective-permute-start.1
  80.4 3.6 %collective-permute-done.1 = bf16[96,384]{1,0:T(8,128)(2,1)S(1)} collective-permute-done((bf16[96,384]{1,0:T(8,128)(2,1)S(1)}, bf16[96,384]{1,0:T(8,128)(2,1)S(1)}, u32[]{:S(2)}, u32[]{:S(2)}) %collective-permute-start.1) | collective-permute-done | bytes 73760 | tf_op jit(solution)/shard_map/ppermute | solution.py:187
  84.1 7.5 %while.87 = (s32[]{:T(128)}, f32[3,256,384]{2,1,0:T(8,128)}, s32[3]{0:T(128)S(1)}, f32[10,768]{1,0:T(8,128)S(1)}, f32[10,48]{1,0:T(8,128)S(1)}, /*index=5*/f32[4...) while((s32[]{:T(128)}, f32[3,256,384]{2,1,0:T(8,128)}, ...), condition=%wide.region_11.12_spmd, body=%wide.region_10.11_spmd.sunk | while | flops 10960902 | bytes 505023 | solution.py:217
  84.1 0.6 dynamic_slice.136
  85.6 1.0 fusion.124
  86.6 0.6 dynamic_slice.136
  88.1 1.0 fusion.124
  89.1 0.6 dynamic_slice.136
  90.6 1.0 fusion.124
  92.9 23.2 %all_gather.16 = bf16[768,384]{1,0:T(8,128)(2,1)S(1)} all-gather(bf16[48,384]{1,0:T(8,128)(2,1)S(1)} %convert_element_type.68), channel_id=1, replica_groups=mesh['groups'=2,'sensor'=16] {'sensor'}, dimensions={0}, use_global_device_ids=true | all-gather | bytes 626688 | tf_op jit(solution)/shard_map/all_gather | solution.py:245
  116.4 1.4 while.91
  117.8 30.6 %reduce-scatter.5.cloned.1.call-done = f32[48,384]{1,0:T(8,128)} async-done(((f32[768,384]{1,0:T(8,128)}), f32[48,384]{1,0:T(8,128)}) %reduce-scatter.5.cloned.1.call-update) | async-done | bytes 73744 | tf_op jit(solution)/shard_map/reduce_scatter | solution.py:216
  148.4 1.0 add_reduce_fusion
  149.7 3.0 %while.92 = (s32[]{:T(128)}, f32[10,48]{1,0:T(8,128)S(1)}, f32[10,768]{1,0:T(8,128)S(1)}, f32[10,768]{1,0:T(8,128)S(1)}, f32[10,48]{1,0:T(8,128)S(1)}, /*index=5...) while((s32[]{:T(128)}, f32[10,48]{1,0:T(8,128)S(1)}, ...), condition=%wide.region_15.16_spmd.clone, body=%wide.region_14.15_spmd.clone.sunk | while | flops 23399876 | bytes 904809 | solution.py:79
  152.7 0.9 copy.46
  154.2 0.8 reshape.89
  155.0 57.8 %psum.7 = f32[96,32]{0,1:T(8,128)} all-reduce(f32[96,32]{0,1:T(8,128)S(1)} %fusion.55), channel_id=1, replica_groups=mesh['groups'=2,'sensor'=16] {'sensor'}, use_global_device_ids=true, to_apply=%region_17.18 | all-reduce | flops 3072 | bytes 24576 | tf_op jit(solution)/shard_map/psum | solution.py:250
  212.8 1.4 copy.47
  (117 shorter events, 11.9 us)
Async XLA Ops:
  7.2 1.5 copy-start
  7.2 141.2 %reduce-scatter.5.cloned.1.call-start = ((), (), s32[]{:S(2)}) async-start(), calls=%async_computation.2 | async-start | bytes 1253376 | tf_op jit(solution)/shard_map/reduce_scatter | solution.py:216
  50.5 3.3 %copy-start.1 = (f32[10,48]{1,0:T(8,128)S(1)}, f32[10,48]{1,0:T(8,128)}, u32[]{:S(2)}) copy-start(f32[10,48]{1,0:T(8,128)} %param.24) | copy-start | bytes 5764
  53.7 2.0 copy-start.5
  76.7 1.8 copy-start.3
  76.7 3.1 %copy-start.4 = (bf16[96,32]{0,1:T(8,128)(2,1)S(1)}, bf16[96,32]{0,1:T(8,128)(2,1)}, u32[]{:S(2)}) copy-start(bf16[96,32]{0,1:T(8,128)(2,1)} %param.28) | copy-start | bytes 18436
  78.1 1.3 collective-permute-start
  79.4 4.6 %collective-permute-start.1 = (bf16[96,384]{1,0:T(8,128)(2,1)S(1)}, bf16[96,384]{1,0:T(8,128)(2,1)S(1)}, u32[]{:S(2)}, u32[]{:S(2)}) collective-permute-start(bf16[96,384]{1,0:T(8,128)(2,1)S(1)} %maximum_select_fusion.3), channel_id=1, source_target_pairs={{0,2},{1,3},{2,0},{3,1},{4,6},{5,7},{6,4},{7,5},{8,10},{9,11},{10,... | collective-permute-start | bytes 221192 | tf_op jit(solution)/shard_map/ppermute | solution.py:187
  84.0 7.7 %collective-permute-start.2 = (bf16[192,384]{1,0:T(8,128)(2,1)S(1)}, bf16[192,384]{1,0:T(8,128)(2,1)S(1)}, u32[]{:S(2)}, u32[]{:S(2)}) collective-permute-start(bf16[192,384]{1,0:T(8,128)(2,1)S(1)} %maximum_select_fusion.2), channel_id=1, source_target_pairs={{0,4},{1,5},{2,6},{3,7},{4,0},{5,1},{6,2},{7,3},{8,12},{9,13},{10,... | collective-permute-start | bytes 442376 | tf_op jit(solution)/shard_map/ppermute | solution.py:187
  91.6 121.1 %reduce-scatter.7.cloned.1.call-start = ((), (), s32[]{:S(2)}) async-start(), calls=%async_computation.3 | async-start | bytes 417792
  91.8 24.4 %collective-permute-start.3 = (bf16[384,384]{1,0:T(8,128)(2,1)S(1)}, bf16[384,384]{1,0:T(8,128)(2,1)S(1)}, u32[]{:S(2)}, u32[]{:S(2)}) collective-permute-start(bf16[384,384]{1,0:T(8,128)(2,1)S(1)} %maximum_select_fusion.1), channel_id=1, source_target_pairs={{0,8},{1,9},{2,10},{3,11},{4,12},{5,13},{6,14},{7,15},{8,0},{9,1},... | collective-permute-start | bytes 884744 | tf_op jit(solution)/shard_map/ppermute | solution.py:187
  152.7 61.5 %copy-start.2 = (f32[10,48]{1,0:T(8,128)}, f32[10,48]{1,0:T(8,128)S(1)}, u32[]{:S(2)}) copy-start(f32[10,48]{1,0:T(8,128)S(1)} %get-tuple-element.696) | copy-start | bytes 5764
Sparse Core Ops, SparseCore 0:
  91.8 56.6 reduce-scatter.4
  153.8 54.7 reduce-scatter.6
